TPU v7x, 256 devices: a whole 4x4x8 slice. The times are simulated.
256 devices in a mesh: dp: 8 (over y, core), ctx: 32 (over x, z).
Axes of the slice: x: 4, y: 4, z: 8, core: 2. Of those that a mesh axis runs over, the one named last changes fastest.
Arguments:
- query_rows: bfloat16 [8, 16384, 1024], P('dp', 'ctx'), may hold values from -6 to 6
- key_rows: bfloat16 [8, 16384, 1024], P('dp', 'ctx'), may hold values from -6 to 6
- value_rows: bfloat16 [8, 16384, 1024], P('dp', 'ctx'), may hold values from -6 to 6
- query_gain: float32 [128], replicated, may hold values from 0.5 to 1.5
- key_gain: float32 [128], replicated, may hold values from 0.5 to 1.5
- selected: int32 [8, 32, 3], P('dp', 'ctx'), may hold values from 0 to 30, as said below
- output_grad: bfloat16 [8, 16384, 1024], P('dp', 'ctx'), may hold values from -6 to 6
Outputs:
- attended: bfloat16 [8, 16384, 1024], P('dp', 'ctx')
- query_grad: bfloat16 [8, 16384, 1024], P('dp', 'ctx')
- key_grad: bfloat16 [8, 16384, 1024], P('dp', 'ctx')
- value_grad: bfloat16 [8, 16384, 1024], P('dp', 'ctx')
- query_gain_grad: float32 [128], replicated
- key_gain_grad: float32 [128], replicated
Inputs may be any that keep to these rules, and one draw needn't show every extreme that they name: selected[b, i, 0] is 0 for every query block i, and selected[b, i, 2] is i - 1 for every i >= 2. Every entry of row i lies in 0 to i, and an entry equal to i names no block. Entries below i are distinct within a row. For i >= 3 every entry is below i.
All inputs are finite; a program needn't handle non-finite values.
Results may differ from a plain program's by a relative error of at most 0.012.
Values may be sent and summed in bfloat16 or wider, within the bound.
A program may use at most 128 MiB of HBM per device.

v0:
```python
import jax
import jax.numpy as jnp
from jax import lax
from jax.sharding import PartitionSpec as P


def head_norm(inputs, gain_vector):
    head_dim = gain_vector.shape[0]
    shaped = inputs.reshape(inputs.shape[:-1] + (inputs.shape[-1] // head_dim, head_dim))
    factor = lax.rsqrt(jnp.mean(shaped * shaped, axis=-1, keepdims=True) + 1e-06)
    return (shaped * factor * gain_vector).reshape(inputs.shape)


def attend(query_block, key_list, value_list, visible_list, grad_block, score_scale):
    weight_list = []
    row_total = 0.0
    for key_block, visible in zip(key_list, visible_list):
        scores = jnp.einsum(
            "qhd,khd->hqk", query_block, key_block, preferred_element_type=jnp.float32
        )
        weights = jnp.exp(score_scale * scores) * visible
        row_total = row_total + jnp.sum(weights, axis=-1)
        weight_list.append(weights)
    prob_list = [(weights / row_total[:, :, None]).astype(jnp.bfloat16) for weights in weight_list]
    accumulated = 0.0
    for prob_block, value_block in zip(prob_list, value_list):
        accumulated = accumulated + jnp.einsum(
            "hqk,khd->qhd", prob_block, value_block, preferred_element_type=jnp.float32
        )
    output = accumulated.astype(jnp.bfloat16)
    row_delta = jnp.einsum("qhd,qhd->hq", grad_block, output, preferred_element_type=jnp.float32)
    query_grad = 0.0
    key_terms = []
    value_terms = []
    for prob_block, key_block, value_block in zip(prob_list, key_list, value_list):
        grad_probs = jnp.einsum(
            "qhd,khd->hqk", grad_block, value_block, preferred_element_type=jnp.float32
        )
        grad_scores = (
            prob_block.astype(jnp.float32) * (grad_probs - row_delta[:, :, None])
        ).astype(jnp.bfloat16)
        value_terms.append(
            jnp.einsum("hqk,qhd->khd", prob_block, grad_block, preferred_element_type=jnp.float32)
        )
        key_terms.append(
            score_scale
            * jnp.einsum(
                "hqk,qhd->khd", grad_scores, query_block, preferred_element_type=jnp.float32
            )
        )
        query_grad = query_grad + score_scale * jnp.einsum(
            "hqk,khd->qhd", grad_scores, key_block, preferred_element_type=jnp.float32
        )
    return (output, query_grad, key_terms, value_terms)


def local(query_rows, key_rows, value_rows, query_gain, key_gain, selected, output_grad):
    ctx_count = lax.axis_size("ctx")
    device_index = lax.axis_index("ctx")
    local_count = selected.shape[1]
    slot_total = selected.shape[2]
    token_count = query_rows.shape[1]
    model_width = query_rows.shape[2]
    head_dim = query_gain.shape[0]
    head_count = model_width // head_dim
    block_size = token_count // local_count
    slice_rows = block_size // ctx_count
    block_count = local_count * ctx_count
    score_scale = head_dim ** (-0.5)

    def heads_view(block_array):
        return block_array.reshape(block_size, head_count, head_dim)

    choice_table = lax.all_gather(selected[0], "ctx", axis=0, tiled=True)
    query_float = query_rows[0].astype(jnp.float32)
    key_float = key_rows[0].astype(jnp.float32)
    query_normed = head_norm(query_float, query_gain).astype(jnp.bfloat16)
    key_normed = head_norm(key_float, key_gain).astype(jnp.bfloat16)
    value_local = value_rows[0]
    holder_keys, holder_values = (
        lax.all_to_all(
            key_normed.reshape(local_count, block_size, model_width),
            "ctx",
            split_axis=1,
            concat_axis=0,
            tiled=True,
        ),
        lax.all_to_all(
            value_local.reshape(local_count, block_size, model_width),
            "ctx",
            split_axis=1,
            concat_axis=0,
            tiled=True,
        ),
    )
    first_slot = 0
    fetched_keys, fetched_values = (
        lax.all_to_all(holder_keys[choice_table], "ctx", split_axis=0, concat_axis=2, tiled=True),
        lax.all_to_all(holder_values[choice_table], "ctx", split_axis=0, concat_axis=2, tiled=True),
    )
    positions = jnp.arange(block_size)
    causal = (positions[None, :] <= positions[:, None]).astype(jnp.float32)[None]
    own_block = device_index * local_count + 0
    chosen = selected[0, 0]
    key_list = [heads_view(key_normed)]
    value_list = [heads_view(value_local)]
    visible_list = [causal]
    for slot_index in range(slot_total):
        fetched_slot = slot_index - first_slot
        key_list.append(heads_view(fetched_keys[0, fetched_slot]))
        value_list.append(heads_view(fetched_values[0, fetched_slot]))
        visible_list.append((chosen[slot_index] != own_block).astype(jnp.float32))
    output, query_grad, key_terms, value_terms = attend(
        heads_view(query_normed),
        key_list,
        value_list,
        visible_list,
        heads_view(output_grad[0, 0:block_size]),
        score_scale,
    )
    outputs = output.reshape(block_size, model_width)
    query_grads = query_grad.reshape(block_size, model_width)
    own_keys = [key_terms[0].reshape(block_size, model_width)]
    own_values = [value_terms[0].reshape(block_size, model_width)]
    remote_keys = [
        jnp.stack([grad_term.astype(jnp.bfloat16) for grad_term in key_terms[1:]]).reshape(
            slot_total, block_size, model_width
        )
    ]
    remote_values = [
        jnp.stack([grad_term.astype(jnp.bfloat16) for grad_term in value_terms[1:]]).reshape(
            slot_total, block_size, model_width
        )
    ]
    remote_key_all = jnp.stack(remote_keys)
    remote_value_all = jnp.stack(remote_values)
    back_keys, back_values = (
        lax.all_to_all(remote_key_all, "ctx", split_axis=2, concat_axis=0, tiled=True),
        lax.all_to_all(remote_value_all, "ctx", split_axis=2, concat_axis=0, tiled=True),
    )
    selector = (choice_table.reshape(-1)[None, :] == jnp.arange(block_count)[:, None]).astype(
        jnp.bfloat16
    )
    summed_keys = jnp.dot(
        selector,
        back_keys.reshape(block_count * slot_total, slice_rows * model_width),
        preferred_element_type=jnp.float32,
    )
    summed_values = jnp.dot(
        selector,
        back_values.reshape(block_count * slot_total, slice_rows * model_width),
        preferred_element_type=jnp.float32,
    )
    summed_keys = summed_keys.reshape(block_count, slice_rows, model_width)
    summed_values = summed_values.reshape(block_count, slice_rows, model_width)
    collected_keys, collected_values = (
        lax.all_to_all(
            summed_keys.astype(jnp.bfloat16), "ctx", split_axis=0, concat_axis=1, tiled=True
        ),
        lax.all_to_all(
            summed_values.astype(jnp.bfloat16), "ctx", split_axis=0, concat_axis=1, tiled=True
        ),
    )
    remote_key_total = collected_keys.astype(jnp.float32)
    remote_value_total = collected_values.astype(jnp.float32)
    key_total = (jnp.stack(own_keys) + remote_key_total).reshape(token_count, model_width)
    value_grad = (
        (jnp.stack(own_values) + remote_value_total)
        .reshape(token_count, model_width)
        .astype(jnp.bfloat16)
    )
    _, query_pull = jax.vjp(head_norm, query_float, query_gain)
    query_grad, query_gain_part = query_pull(query_grads)
    _, key_pull = jax.vjp(head_norm, key_float, key_gain)
    key_grad, key_gain_part = key_pull(key_total)
    query_gain_grad, key_gain_grad = lax.psum((query_gain_part, key_gain_part), ("dp", "ctx"))
    return (
        outputs[None],
        query_grad.astype(jnp.bfloat16)[None],
        key_grad.astype(jnp.bfloat16)[None],
        value_grad[None],
        query_gain_grad,
        key_gain_grad,
    )


def solution(mesh):
    in_specs = (
        P("dp", "ctx", None),
        P("dp", "ctx", None),
        P("dp", "ctx", None),
        P(),
        P(),
        P("dp", "ctx", None),
        P("dp", "ctx", None),
    )
    out_specs = (
        P("dp", "ctx", None),
        P("dp", "ctx", None),
        P("dp", "ctx", None),
        P("dp", "ctx", None),
        P(),
        P(),
    )
    return jax.shard_map(local, mesh=mesh, in_specs=in_specs, out_specs=out_specs, check_vma=False)
```

profile of v0, /device:TPU:1, one launch (start us, length us, event | category | flops | bytes accessed | tf_op | source)
XLA Modules:
  0.0 716.8 jit_solution(10691990284044521353)
XLA Ops:
  13.3 9.1 %reduce.7 = bf16[512,1024]{1,0:T(8,128)(2,1)} reduce(bf16[512,1,1024]{2,1,0:T(2,128)(2,1)} %bitcast.237, bf16[]{:T(256)} %broadcast.153), dimensions={1}, to_apply=%bitcast.200.reduce_sub_computation | reduce | bytes 2097154
  25.0 12.2 %all-to-all-start = ((bf16[32,2,8192]{2,1,0:T(2,128)(2,1)}), bf16[32,2,8192]{2,1,0:T(2,128)(2,1)}, u32[]{:S(2)}, u32[]{:S(2)}) async-start(bf16[32,2,8192]{2,1,0:T(2,128)(2,1)} %reshape.270), calls=%async_computation | async-start | bytes 2097152 | tf_op jit(solution)/shard_map/all_to_all | solution.py:81
  40.1 8.0 %reduce.6 = bf16[512,1024]{1,0:T(8,128)(2,1)S(1)} reduce(bf16[512,1,1024]{2,1,0:T(2,128)(2,1)} %bitcast.238, bf16[]{:T(256)} %broadcast.153), dimensions={1}, to_apply=%bitcast.199.reduce_sub_computation | reduce | bytes 2097154
  49.7 12.0 %all-to-all-done = bf16[32,2,8192]{2,1,0:T(2,128)(2,1)} async-done(((bf16[32,2,8192]{2,1,0:T(2,128)(2,1)}), bf16[32,2,8192]{2,1,0:T(2,128)(2,1)}, u32[]{:S(2)}, u32[]{:S(2)}) %all-to-all-start) | async-done | bytes 1048608 | tf_op jit(solution)/shard_map/all_to_all | solution.py:81
  61.7 8.7 %all-to-all-start.2 = ((bf16[32,2,8192]{2,1,0:T(2,128)(2,1)}), bf16[32,2,8192]{2,1,0:T(2,128)(2,1)}, u32[]{:S(2)}, u32[]{:S(2)}) async-start(bf16[32,2,8192]{2,1,0:T(2,128)(2,1)} %reshape.268), calls=%async_computation.2 | async-start | bytes 2097152 | tf_op jit(solution)/shard_map/all_to_all | solution.py:88
  70.5 48.7 %all-gather = s32[32,1,3]{2,1,0:T(1,128)S(1)} all-gather(s32[1,1,3]{2,1,0:T(1,128)S(1)} %copy-done.32), channel_id=2, replica_groups=mesh['dp'=8,'ctx'=32] {'ctx'}, dimensions={0}, use_global_device_ids=true | all-gather | bytes 396 | tf_op jit(solution)/shard_map/all_gather | solution.py:74
  119.5 5.8 reshape.271
  129.8 5.3 all-to-all-start.1
  135.1 5.8 reshape.269
  145.5 54.6 %all-to-all-done.1 = bf16[32,3,16,1024]{3,2,1,0:T(8,128)(2,1)} async-done(((bf16[32,3,16,1024]{3,2,1,0:T(8,128)(2,1)}), bf16[32,3,16,1024]{3,2,1,0:T(8,128)(2,1)}, u32[]{:S(2)}, u32[]{:S(2)}) %all-to-all-start.1) | async-done | bytes 3145760 | tf_op jit(solution)/shard_map/all_to_all | solution.py:98
  200.1 5.4 all-to-all-start.3
  217.4 4.4 fusion.3
  232.8 34.6 %all-to-all-done.3 = bf16[32,3,16,1024]{3,2,1,0:T(8,128)(2,1)} async-done(((bf16[32,3,16,1024]{3,2,1,0:T(8,128)(2,1)}), bf16[32,3,16,1024]{3,2,1,0:T(8,128)(2,1)}, u32[]{:S(2)}, u32[]{:S(2)}) %all-to-all-start.3) | async-done | bytes 3145760 | tf_op jit(solution)/shard_map/all_to_all | solution.py:99
  278.4 6.3 fusion.6
  284.8 5.1 fusion.5
  289.9 5.0 fusion.4
  295.0 11.9 %divide_convert_fusion.3 = (bf16[8,512,512]{1,2,0:T(8,128)(2,1)S(1)}, bf16[8,512,512]{1,2,0:T(8,128)(2,1)S(1)}, bf16[8,512,512]{1,2,0:T(8,128)(2,1)S(1)}, bf16[8,512,512]{1,2,0:T(8,128)(2,1)S(1)}) fusion(f32[8,512,512]{1,2,0:T(8,128)S(1)} %bitcast.207, f32[8,512]{1,0:T(8,128)S(1)} %add_add_fusion.2, f32[512,512]{0,1:T(8,128)} %copy-done.14, ...), kind=kLoop, calls=%fused_computation.12 | loop fusion | flops 33554432 | bytes 51396620 | tf_op jit(solution)/shard_map/convert_element_type | solution.py:24
  321.4 4.0 fusion.2
  325.5 3.3 fusion.1
  336.6 6.0 copy.538
  342.6 4.6 multiply_convert_fusion.2
  347.3 6.0 copy.539
  353.3 4.6 multiply_convert_fusion.1
  358.0 6.2 copy.540
  364.1 9.6 %pad_maximum_fusion = bf16[1,3,512,1024]{3,1,0,2:T(4,128)(2,1)} fusion(bf16[1,1,512,1024]{3,1,0,2:T(2,128)(2,1)} %copy.540, bf16[1,1,512,1024]{3,1,0,2:T(2,128)(2,1)} %copy.539, bf16[1,1,512,1024]{3,1,0,2:T(2,128)(2,1)} %copy.538), kind=kLoop, calls=%fused_computation.21 | loop fusion | flops 9437184 | bytes 6291456 | tf_op jit(solution)/shard_map/stack | solution.py:126
  373.8 7.3 %all-to-all-start.4 = ((bf16[1,3,512,1024]{3,1,0,2:T(4,128)(2,1)}), bf16[1,3,512,1024]{3,1,0,2:T(4,128)(2,1)}, u32[]{:S(2)}, u32[]{:S(2)}) async-start(bf16[1,3,512,1024]{3,1,0,2:T(4,128)(2,1)} %pad_maximum_fusion), calls=%async_computation.4 | async-start | bytes 8388608 | tf_op jit(solution)/shard_map/all_to_all | solution.py:138
  381.1 4.6 convolution_convert_fusion.2
  385.7 6.1 copy.556
  391.8 4.6 convolution_convert_fusion.1
  396.4 6.0 copy.557
  402.4 4.6 convolution_convert_fusion
  407.1 6.1 copy.558
  413.2 9.7 %pad_maximum_fusion.1 = bf16[1,3,512,1024]{3,1,0,2:T(4,128)(2,1)} fusion(bf16[1,1,512,1024]{3,1,0,2:T(2,128)(2,1)} %copy.558, bf16[1,1,512,1024]{3,1,0,2:T(2,128)(2,1)} %copy.557, bf16[1,1,512,1024]{3,1,0,2:T(2,128)(2,1)} %copy.556), kind=kLoop, calls=%fused_computation.22 | loop fusion | flops 9437184 | bytes 6291456 | tf_op jit(solution)/shard_map/stack | solution.py:131
  422.9 42.1 %all-to-all-done.4 = bf16[1,3,512,1024]{3,1,0,2:T(4,128)(2,1)} async-done(((bf16[1,3,512,1024]{3,1,0,2:T(4,128)(2,1)}), bf16[1,3,512,1024]{3,1,0,2:T(4,128)(2,1)}, u32[]{:S(2)}, u32[]{:S(2)}) %all-to-all-start.4) | async-done | bytes 3145760 | tf_op jit(solution)/shard_map/all_to_all | solution.py:138
  465.0 9.8 %all-to-all-start.6 = ((bf16[1,3,512,1024]{3,1,0,2:T(4,128)(2,1)}), bf16[1,3,512,1024]{3,1,0,2:T(4,128)(2,1)}, u32[]{:S(2)}, u32[]{:S(2)}) async-start(bf16[1,3,512,1024]{3,1,0,2:T(4,128)(2,1)} %pad_maximum_fusion.1), calls=%async_computation.6 | async-start | bytes 8388608 | tf_op jit(solution)/shard_map/all_to_all | solution.py:139
  476.1 4.6 fusion.44
  480.7 3.4 copy.541
  484.5 3.6 fusion.20
  489.7 71.2 %all-to-all-done.6 = bf16[1,3,512,1024]{3,1,0,2:T(4,128)(2,1)} async-done(((bf16[1,3,512,1024]{3,1,0,2:T(4,128)(2,1)}), bf16[1,3,512,1024]{3,1,0,2:T(4,128)(2,1)}, u32[]{:S(2)}, u32[]{:S(2)}) %all-to-all-start.6) | async-done | bytes 3145760 | tf_op jit(solution)/shard_map/all_to_all | solution.py:139
  560.9 7.3 %all-to-all-start.5 = ((bf16[32,16,1024]{2,1,0:T(8,128)(2,1)}), bf16[32,16,1024]{2,1,0:T(8,128)(2,1)}, u32[]{:S(2)}, u32[]{:S(2)}) async-start(bf16[32,16,1024]{2,1,0:T(8,128)(2,1)} %copy.544), calls=%async_computation.5 | async-start | bytes 2097152 | tf_op jit(solution)/shard_map/all_to_all | solution.py:157
  568.2 3.4 fusion.45
  581.0 3.4 copy.559
  584.8 3.6 fusion.23
  590.0 9.6 %all-to-all-start.7 = ((bf16[32,16,1024]{2,1,0:T(8,128)(2,1)}), bf16[32,16,1024]{2,1,0:T(8,128)(2,1)S(1)}, u32[]{:S(2)}, u32[]{:S(2)}) async-start(bf16[32,16,1024]{2,1,0:T(8,128)(2,1)} %copy.562), calls=%async_computation.7 | async-start | bytes 2097152 | tf_op jit(solution)/shard_map/all_to_all | solution.py:160
  599.6 5.0 fusion.46
  607.6 3.9 fusion.15
  620.9 5.2 multiply_reduce_fusion.1
  630.0 85.0 %all-reduce = (f32[128]{0:T(128)}, f32[128]{0:T(128)}) all-reduce(f32[128]{0:T(128)S(1)} %get-tuple-element.56, f32[128]{0:T(128)S(1)} %get-tuple-element.54), channel_id=1, replica_groups=mesh['dp'=8,'ctx'=32] {'dp','ctx'}, use_global_device_ids=true, to_apply=%region_9.0 | all-reduce | flops 256 | bytes 2048 | tf_op jit(solution)/shard_map/psum | solution.py:176
  (149 shorter events, 115.4 us)
Async XLA Ops:
  3.3 4.5 copy-start.31
  3.3 4.5 copy-start.26
  13.3 23.9 %copy-start.27 = (bf16[1,512,1024]{2,1,0:T(8,128)(2,1)S(1)}, bf16[1,512,1024]{2,1,0:T(8,128)(2,1)}, u32[]{:S(2)}) copy-start(bf16[1,512,1024]{2,1,0:T(8,128)(2,1)} %param.9) | copy-start | bytes 3145732
  25.0 36.8 %all-to-all-start = ((bf16[32,2,8192]{2,1,0:T(2,128)(2,1)}), bf16[32,2,8192]{2,1,0:T(2,128)(2,1)}, u32[]{:S(2)}, u32[]{:S(2)}) async-start(bf16[32,2,8192]{2,1,0:T(2,128)(2,1)} %reshape.270), calls=%async_computation | async-start | bytes 2097152 | tf_op jit(solution)/shard_map/all_to_all | solution.py:81
  40.1 30.4 %copy-start.32 = (s32[1,1,3]{2,1,0:T(1,128)S(1)}, s32[1,1,3]{2,1,0:T(1,128)}, u32[]{:S(2)}) copy-start(s32[1,1,3]{2,1,0:T(1,128)} %param.12) | copy-start | bytes 40
  61.7 68.1 %all-to-all-start.2 = ((bf16[32,2,8192]{2,1,0:T(2,128)(2,1)}), bf16[32,2,8192]{2,1,0:T(2,128)(2,1)}, u32[]{:S(2)}, u32[]{:S(2)}) async-start(bf16[32,2,8192]{2,1,0:T(2,128)(2,1)} %reshape.268), calls=%async_computation.2 | async-start | bytes 2097152 | tf_op jit(solution)/shard_map/all_to_all | solution.py:88
  129.8 70.3 %all-to-all-start.1 = ((bf16[32,3,16,1024]{3,2,1,0:T(8,128)(2,1)}), bf16[32,3,16,1024]{3,2,1,0:T(8,128)(2,1)}, u32[]{:S(2)}, u32[]{:S(2)}) async-start(bf16[32,3,16,1024]{3,2,1,0:T(8,128)(2,1)} %bitcast.215), calls=%async_computation.1 | async-start | bytes 6291456 | tf_op jit(solution)/shard_map/all_to_all | solution.py:98
  200.1 67.3 %all-to-all-start.3 = ((bf16[32,3,16,1024]{3,2,1,0:T(8,128)(2,1)}), bf16[32,3,16,1024]{3,2,1,0:T(8,128)(2,1)}, u32[]{:S(2)}, u32[]{:S(2)}) async-start(bf16[32,3,16,1024]{3,2,1,0:T(8,128)(2,1)} %bitcast.214), calls=%async_computation.3 | async-start | bytes 6291456 | tf_op jit(solution)/shard_map/all_to_all | solution.py:99
  205.5 1.9 copy-start.29
  207.4 4.2 copy-start.28
  207.4 4.5 copy-start.30
  212.1 3.2 copy-start.19
  212.1 3.2 copy-start.33
  212.8 4.5 copy-start.8
  213.0 8.8 %copy-start.14 = (f32[512,512]{0,1:T(8,128)}, f32[512,512]{0,1:T(8,128)S(1)}, u32[]{:S(2)}) copy-start(f32[512,512]{0,1:T(8,128)S(1)} %fusion.26) | copy-start | bytes 3145732
  278.4 6.3 copy-start.21
  284.8 5.1 copy-start.22
  284.8 10.1 %slice-start = ((s8[8388608]{0:T(1024)(128)(4,1)}), s8[4194304]{0:T(1024)(128)(4,1)S(1)}, s32[]{:S(2)}) async-start(s8[8388608]{0:T(1024)(128)(4,1)} %bitcast.206), calls=%async_computation.8 | async-start | bytes 8388608
  289.9 5.1 slice-start.1
  306.9 3.9 copy-start.2
  306.9 5.8 copy-start.4
  306.9 5.8 copy-start.6
  306.9 6.3 copy-start
  306.9 3.1 copy-start.15
  310.0 2.0 copy-start.17
  321.4 4.0 copy-start.5
  321.4 4.1 copy-start.16
  325.5 8.7 %copy-start.11 = (bf16[8,512,512]{1,2,0:T(8,128)(2,1)}, bf16[8,512,512]{1,2,0:T(8,128)(2,1)S(1)}, u32[]{:S(2)}) copy-start(bf16[8,512,512]{1,2,0:T(8,128)(2,1)S(1)} %fusion.2) | copy-start | bytes 12582916
  325.5 5.1 copy-start.3
  325.5 5.4 copy-start.18
  373.8 91.2 %all-to-all-start.4 = ((bf16[1,3,512,1024]{3,1,0,2:T(4,128)(2,1)}), bf16[1,3,512,1024]{3,1,0,2:T(4,128)(2,1)}, u32[]{:S(2)}, u32[]{:S(2)}) async-start(bf16[1,3,512,1024]{3,1,0,2:T(4,128)(2,1)} %pad_maximum_fusion), calls=%async_computation.4 | async-start | bytes 8388608 | tf_op jit(solution)/shard_map/all_to_all | solution.py:138
  465.0 95.9 %all-to-all-start.6 = ((bf16[1,3,512,1024]{3,1,0,2:T(4,128)(2,1)}), bf16[1,3,512,1024]{3,1,0,2:T(4,128)(2,1)}, u32[]{:S(2)}, u32[]{:S(2)}) async-start(bf16[1,3,512,1024]{3,1,0,2:T(4,128)(2,1)} %pad_maximum_fusion.1), calls=%async_computation.6 | async-start | bytes 8388608 | tf_op jit(solution)/shard_map/all_to_all | solution.py:139
  560.9 29.1 %all-to-all-start.5 = ((bf16[32,16,1024]{2,1,0:T(8,128)(2,1)}), bf16[32,16,1024]{2,1,0:T(8,128)(2,1)}, u32[]{:S(2)}, u32[]{:S(2)}) async-start(bf16[32,16,1024]{2,1,0:T(8,128)(2,1)} %copy.544), calls=%async_computation.5 | async-start | bytes 2097152 | tf_op jit(solution)/shard_map/all_to_all | solution.py:157
  568.2 3.7 copy-start.1
  572.0 1.6 copy-start.9
  572.0 3.7 copy-start.23
  573.6 2.1 copy-start.12
  573.6 3.3 copy-start.7
  573.6 4.5 copy-start.13
  573.6 4.7 copy-start.20
  590.0 125.0 %all-to-all-start.7 = ((bf16[32,16,1024]{2,1,0:T(8,128)(2,1)}), bf16[32,16,1024]{2,1,0:T(8,128)(2,1)S(1)}, u32[]{:S(2)}, u32[]{:S(2)}) async-start(bf16[32,16,1024]{2,1,0:T(8,128)(2,1)} %copy.562), calls=%async_computation.7 | async-start | bytes 2097152 | tf_op jit(solution)/shard_map/all_to_all | solution.py:160
  607.6 6.2 copy-start.25
  620.9 5.2 copy-start.10
  626.1 88.9 %copy-start.24 = (f32[1,512,1024]{2,1,0:T(8,128)S(1)}, f32[1,512,1024]{2,1,0:T(8,128)}, u32[]{:S(2)}) copy-start(f32[1,512,1024]{2,1,0:T(8,128)} %copy.563) | copy-start | bytes 6291460
where the time goes:
time: 727 us; the launch traced here: 717 us
  waiting for transfers between devices  215 us (30%)
  local copies, waits for them, and re-layouts  138 us (19%)
  blocking collectives  134 us (18%)
  matrix products  94.3 us (13%)
  other arithmetic  66.9 us (9%)
  starting transfers between devices  65.5 us (9%)
    psum x1, blocking collectives, local(): lax.psum((query_gain_part, key_gain_part), ('dp', 'ctx'))  85 us
    all_to_all x1, waiting for transfers between devices, local(): lax.all_to_all(remote_value_all, 'ctx', split_axis=2, concat_axis=0, tile...  71.2 us
    all_to_all x1, waiting for transfers between devices, local(): lax.all_to_all(holder_keys[choice_table], 'ctx', split_axis=0, concat_axi...  54.6 us
    all_gather x1, blocking collectives, local(): choice_table = lax.all_gather(selected[0], 'ctx', axis=0, tiled=True)  48.7 us
    unnamed x88, local copies, waits for them, and re-layouts  44.6 us
    all_to_all x1, waiting for transfers between devices, local(): lax.all_to_all(remote_key_all, 'ctx', split_axis=2, concat_axis=0, tiled=...  42.1 us
    all_to_all x1, waiting for transfers between devices, local(): lax.all_to_all(holder_values[choice_table], 'ctx', split_axis=0, concat_a...  34.6 us
    unnamed x5, other arithmetic  21.1 us
  transfers between devices with their start and end apart: 8, of which 5 were waited for; matrix products, arithmetic and copies ran while one was open for 23% of the time, Pallas kernels for 0%

commit v1 on v0

--- a/solution.py
+++ b/solution.py
@@ -71,7 +71,11 @@
     def heads_view(block_array):
         return block_array.reshape(block_size, head_count, head_dim)
 
-    choice_table = lax.all_gather(selected[0], "ctx", axis=0, tiled=True)
+    count = lax.axis_size("ctx")
+    repeats = [count if d == 0 else 1 for d in range(selected[0].ndim)]
+    choice_table = lax.all_to_all(
+        jnp.tile(selected[0], repeats), "ctx", split_axis=0, concat_axis=0, tiled=True
+    )
     query_float = query_rows[0].astype(jnp.float32)
     key_float = key_rows[0].astype(jnp.float32)
     query_normed = head_norm(query_float, query_gain).astype(jnp.bfloat16)

time: 727 us -> 737 us (1.014)
  blocking collectives: 134 us -> 77.5 us
  waiting for transfers between devices: 215 us -> 266 us
  starting transfers between devices: 65.5 us -> 78.8 us
    all_gather x1 -> x0, blocking collectives: 48.7 us -> none  [local(): choice_table = lax.all_gather(selected[0], 'ctx', axis=0, tiled=True)]
    all_to_all x1, waiting for transfers between devices: 0.01 us -> 14.2 us  [local(): lax.all_to_all(value_local.reshape(local_count, block_size, model_width),...]
    all_to_all x0 -> x1, starting transfers between devices: none -> 11.9 us  [local(): lax.all_to_all(jnp.tile(selected[0], repeats), 'ctx', split_axis=0, conca...]
    all_to_all x1, waiting for transfers between devices: 34.6 us -> 43.9 us  [local(): lax.all_to_all(holder_values[choice_table], 'ctx', split_axis=0, concat_a...]
    all_to_all x1, waiting for transfers between devices: 42.1 us -> 50.9 us  [local(): lax.all_to_all(remote_key_all, 'ctx', split_axis=2, concat_axis=0, tiled=...]
    all_to_all x1, waiting for transfers between devices: 54.6 us -> 62.9 us  [local(): lax.all_to_all(holder_keys[choice_table], 'ctx', split_axis=0, concat_axi...]
    all_to_all x1, waiting for transfers between devices: 71.2 us -> 78.8 us  [local(): lax.all_to_all(remote_value_all, 'ctx', split_axis=2, concat_axis=0, tile...]
    psum x1, blocking collectives: 85 us -> 77.5 us  [local(): lax.psum((query_gain_part, key_gain_part), ('dp', 'ctx'))]
  transfers between devices with their start and end apart: 8 -> 9, of which waited for: 5 -> 7; matrix products, arithmetic and copies ran while one was open for 23% -> 26% of each run, Pallas kernels for 0% -> 0%
where the time goes in v1:
time: 737 us; the launch traced here: 726 us
  waiting for transfers between devices  266 us (36%)
  local copies, waits for them, and re-layouts  139 us (19%)
  matrix products  94.4 us (13%)
  starting transfers between devices  78.8 us (11%)
  blocking collectives  77.5 us (11%)
  other arithmetic  66.9 us (9%)
    all_to_all x1, waiting for transfers between devices, local(): lax.all_to_all(remote_value_all, 'ctx', split_axis=2, concat_axis=0, tile...  78.8 us
    psum x1, blocking collectives, local(): lax.psum((query_gain_part, key_gain_part), ('dp', 'ctx'))  77.5 us
    all_to_all x1, waiting for transfers between devices, local(): lax.all_to_all(holder_keys[choice_table], 'ctx', split_axis=0, concat_axi...  62.9 us
    all_to_all x1, waiting for transfers between devices, local(): lax.all_to_all(remote_key_all, 'ctx', split_axis=2, concat_axis=0, tiled=...  50.9 us
    unnamed x88, local copies, waits for them, and re-layouts  44.5 us
    all_to_all x1, waiting for transfers between devices, local(): lax.all_to_all(holder_values[choice_table], 'ctx', split_axis=0, concat_a...  43.9 us
    unnamed x5, other arithmetic  21.1 us
    dot_general x4, matrix products, attend(): jnp.einsum('qhd,khd->hqk', query_block, key_block, preferred_element_type...  20.9 us
  transfers between devices with their start and end apart: 9, of which 7 were waited for; matrix products, arithmetic and copies ran while one was open for 26% of the time, Pallas kernels for 0%

profile of v1, /device:TPU:1, one launch (start us, length us, event | category | flops | bytes accessed | tf_op | source)
XLA Modules:
  0.0 726.3 jit_solution(17885337512827676164)
XLA Ops:
  1.9 11.9 %all-to-all-start.1 = ((s32[32,1,3]{2,1,0:T(1,128)}), s32[32,1,3]{2,1,0:T(1,128)S(1)}, u32[]{:S(2)}, u32[]{:S(2)}) async-start(s32[32,1,3]{2,1,0:T(1,128)} %tile.2), calls=%async_computation.1 | async-start | bytes 32768 | tf_op jit(solution)/shard_map/all_to_all | solution.py:76
  26.4 9.1 %reduce.7 = bf16[512,1024]{1,0:T(8,128)(2,1)} reduce(bf16[512,1,1024]{2,1,0:T(2,128)(2,1)} %bitcast.240, bf16[]{:T(256)} %broadcast.173), dimensions={1}, to_apply=%bitcast.203.reduce_sub_computation | reduce | bytes 2097154
  38.1 9.5 %all-to-all-start = ((bf16[32,2,8192]{2,1,0:T(2,128)(2,1)}), bf16[32,2,8192]{2,1,0:T(2,128)(2,1)}, u32[]{:S(2)}, u32[]{:S(2)}) async-start(bf16[32,2,8192]{2,1,0:T(2,128)(2,1)} %reshape.304), calls=%async_computation | async-start | bytes 2097152 | tf_op jit(solution)/shard_map/all_to_all | solution.py:85
  50.6 8.0 %reduce.6 = bf16[512,1024]{1,0:T(8,128)(2,1)S(1)} reduce(bf16[512,1,1024]{2,1,0:T(2,128)(2,1)} %bitcast.241, bf16[]{:T(256)} %broadcast.173), dimensions={1}, to_apply=%bitcast.202.reduce_sub_computation | reduce | bytes 2097154
  60.2 12.1 %all-to-all-done = bf16[32,2,8192]{2,1,0:T(2,128)(2,1)} async-done(((bf16[32,2,8192]{2,1,0:T(2,128)(2,1)}), bf16[32,2,8192]{2,1,0:T(2,128)(2,1)}, u32[]{:S(2)}, u32[]{:S(2)}) %all-to-all-start) | async-done | bytes 1048608 | tf_op jit(solution)/shard_map/all_to_all | solution.py:85
  72.2 8.7 %all-to-all-start.3 = ((bf16[32,2,8192]{2,1,0:T(2,128)(2,1)}), bf16[32,2,8192]{2,1,0:T(2,128)(2,1)}, u32[]{:S(2)}, u32[]{:S(2)}) async-start(bf16[32,2,8192]{2,1,0:T(2,128)(2,1)} %reshape.302), calls=%async_computation.3 | async-start | bytes 2097152 | tf_op jit(solution)/shard_map/all_to_all | solution.py:92
  81.2 5.8 reshape.305
  91.5 14.2 %all-to-all-done.3 = bf16[32,2,8192]{2,1,0:T(2,128)(2,1)} async-done(((bf16[32,2,8192]{2,1,0:T(2,128)(2,1)}), bf16[32,2,8192]{2,1,0:T(2,128)(2,1)}, u32[]{:S(2)}, u32[]{:S(2)}) %all-to-all-start.3) | async-done | bytes 1048608 | tf_op jit(solution)/shard_map/all_to_all | solution.py:92
  105.7 8.5 %all-to-all-start.2 = ((bf16[32,3,16,1024]{3,2,1,0:T(8,128)(2,1)}), bf16[32,3,16,1024]{3,2,1,0:T(8,128)(2,1)}, u32[]{:S(2)}, u32[]{:S(2)}) async-start(bf16[32,3,16,1024]{3,2,1,0:T(8,128)(2,1)} %bitcast.218), calls=%async_computation.2 | async-start | bytes 6291456 | tf_op jit(solution)/shard_map/all_to_all | solution.py:102
  114.2 5.8 reshape.303
  124.6 62.9 %all-to-all-done.2 = bf16[32,3,16,1024]{3,2,1,0:T(8,128)(2,1)} async-done(((bf16[32,3,16,1024]{3,2,1,0:T(8,128)(2,1)}), bf16[32,3,16,1024]{3,2,1,0:T(8,128)(2,1)}, u32[]{:S(2)}, u32[]{:S(2)}) %all-to-all-start.2) | async-done | bytes 3145760 | tf_op jit(solution)/shard_map/all_to_all | solution.py:102
  187.5 6.0 all-to-all-start.4
  205.4 4.4 fusion.3
  220.9 43.9 %all-to-all-done.4 = bf16[32,3,16,1024]{3,2,1,0:T(8,128)(2,1)} async-done(((bf16[32,3,16,1024]{3,2,1,0:T(8,128)(2,1)}), bf16[32,3,16,1024]{3,2,1,0:T(8,128)(2,1)}, u32[]{:S(2)}, u32[]{:S(2)}) %all-to-all-start.4) | async-done | bytes 3145760 | tf_op jit(solution)/shard_map/all_to_all | solution.py:103
  275.9 6.3 fusion.6
  282.2 5.1 fusion.5
  287.3 5.1 fusion.4
  292.4 11.9 %divide_convert_fusion.3 = (bf16[8,512,512]{1,2,0:T(8,128)(2,1)S(1)}, bf16[8,512,512]{1,2,0:T(8,128)(2,1)S(1)}, bf16[8,512,512]{1,2,0:T(8,128)(2,1)S(1)}, bf16[8,512,512]{1,2,0:T(8,128)(2,1)S(1)}) fusion(f32[8,512,512]{1,2,0:T(8,128)S(1)} %bitcast.210, f32[8,512]{1,0:T(8,128)S(1)} %add_add_fusion.2, f32[512,512]{0,1:T(8,128)} %copy-done.14, ...), kind=kLoop, calls=%fused_computation.12 | loop fusion | flops 33554432 | bytes 51396620 | tf_op jit(solution)/shard_map/convert_element_type | solution.py:24
  318.9 4.0 fusion.2
  334.1 6.0 copy.538
  340.1 4.6 multiply_convert_fusion.2
  344.7 6.0 copy.539
  350.8 4.6 multiply_convert_fusion.1
  355.4 6.2 copy.540
  361.6 9.6 %pad_maximum_fusion = bf16[1,3,512,1024]{3,1,0,2:T(4,128)(2,1)} fusion(bf16[1,1,512,1024]{3,1,0,2:T(2,128)(2,1)} %copy.540, bf16[1,1,512,1024]{3,1,0,2:T(2,128)(2,1)} %copy.539, bf16[1,1,512,1024]{3,1,0,2:T(2,128)(2,1)} %copy.538), kind=kLoop, calls=%fused_computation.21 | loop fusion | flops 9437184 | bytes 6291456 | tf_op jit(solution)/shard_map/stack | solution.py:130
  371.2 7.6 %all-to-all-start.5 = ((bf16[1,3,512,1024]{3,1,0,2:T(4,128)(2,1)}), bf16[1,3,512,1024]{3,1,0,2:T(4,128)(2,1)}, u32[]{:S(2)}, u32[]{:S(2)}) async-start(bf16[1,3,512,1024]{3,1,0,2:T(4,128)(2,1)} %pad_maximum_fusion), calls=%async_computation.5 | async-start | bytes 8388608 | tf_op jit(solution)/shard_map/all_to_all | solution.py:142
  378.9 4.6 convolution_convert_fusion.2
  383.5 6.1 copy.556
  389.6 4.6 convolution_convert_fusion.1
  394.2 6.1 copy.557
  400.3 4.6 convolution_convert_fusion
  404.9 6.1 copy.558
  411.0 9.7 %pad_maximum_fusion.1 = bf16[1,3,512,1024]{3,1,0,2:T(4,128)(2,1)} fusion(bf16[1,1,512,1024]{3,1,0,2:T(2,128)(2,1)} %copy.558, bf16[1,1,512,1024]{3,1,0,2:T(2,128)(2,1)} %copy.557, bf16[1,1,512,1024]{3,1,0,2:T(2,128)(2,1)} %copy.556), kind=kLoop, calls=%fused_computation.22 | loop fusion | flops 9437184 | bytes 6291456 | tf_op jit(solution)/shard_map/stack | solution.py:135
  420.7 50.9 %all-to-all-done.5 = bf16[1,3,512,1024]{3,1,0,2:T(4,128)(2,1)} async-done(((bf16[1,3,512,1024]{3,1,0,2:T(4,128)(2,1)}), bf16[1,3,512,1024]{3,1,0,2:T(4,128)(2,1)}, u32[]{:S(2)}, u32[]{:S(2)}) %all-to-all-start.5) | async-done | bytes 3145760 | tf_op jit(solution)/shard_map/all_to_all | solution.py:142
  471.6 9.5 %all-to-all-start.7 = ((bf16[1,3,512,1024]{3,1,0,2:T(4,128)(2,1)}), bf16[1,3,512,1024]{3,1,0,2:T(4,128)(2,1)}, u32[]{:S(2)}, u32[]{:S(2)}) async-start(bf16[1,3,512,1024]{3,1,0,2:T(4,128)(2,1)} %pad_maximum_fusion.1), calls=%async_computation.7 | async-start | bytes 8388608 | tf_op jit(solution)/shard_map/all_to_all | solution.py:143
  482.4 4.6 fusion.44
  487.0 3.4 copy.541
  490.8 3.6 fusion.20
  496.0 78.8 %all-to-all-done.7 = bf16[1,3,512,1024]{3,1,0,2:T(4,128)(2,1)} async-done(((bf16[1,3,512,1024]{3,1,0,2:T(4,128)(2,1)}), bf16[1,3,512,1024]{3,1,0,2:T(4,128)(2,1)}, u32[]{:S(2)}, u32[]{:S(2)}) %all-to-all-start.7) | async-done | bytes 3145760 | tf_op jit(solution)/shard_map/all_to_all | solution.py:143
  574.8 8.4 %all-to-all-start.6 = ((bf16[32,16,1024]{2,1,0:T(8,128)(2,1)}), bf16[32,16,1024]{2,1,0:T(8,128)(2,1)}, u32[]{:S(2)}, u32[]{:S(2)}) async-start(bf16[32,16,1024]{2,1,0:T(8,128)(2,1)} %copy.544), calls=%async_computation.6 | async-start | bytes 2097152 | tf_op jit(solution)/shard_map/all_to_all | solution.py:161
  583.2 3.4 fusion.45
  596.0 3.4 copy.559
  599.8 3.6 fusion.23
  608.0 8.7 %all-to-all-start.8 = ((bf16[32,16,1024]{2,1,0:T(8,128)(2,1)}), bf16[32,16,1024]{2,1,0:T(8,128)(2,1)S(1)}, u32[]{:S(2)}, u32[]{:S(2)}) async-start(bf16[32,16,1024]{2,1,0:T(8,128)(2,1)} %copy.562), calls=%async_computation.8 | async-start | bytes 2097152 | tf_op jit(solution)/shard_map/all_to_all | solution.py:164
  616.7 5.0 fusion.46
  624.6 3.9 fusion.15
  637.9 5.2 multiply_reduce_fusion.1
  647.0 77.5 %all-reduce = (f32[128]{0:T(128)}, f32[128]{0:T(128)}) all-reduce(f32[128]{0:T(128)S(1)} %get-tuple-element.56, f32[128]{0:T(128)S(1)} %get-tuple-element.54), channel_id=1, replica_groups=mesh['dp'=8,'ctx'=32] {'dp','ctx'}, use_global_device_ids=true, to_apply=%region_9.0 | all-reduce | flops 256 | bytes 2048 | tf_op jit(solution)/shard_map/psum | solution.py:180
  (151 shorter events, 122.9 us)
Async XLA Ops:
  1.9 36.2 %all-to-all-start.1 = ((s32[32,1,3]{2,1,0:T(1,128)}), s32[32,1,3]{2,1,0:T(1,128)S(1)}, u32[]{:S(2)}, u32[]{:S(2)}) async-start(s32[32,1,3]{2,1,0:T(1,128)} %tile.2), calls=%async_computation.1 | async-start | bytes 32768 | tf_op jit(solution)/shard_map/all_to_all | solution.py:76
  16.5 4.5 copy-start.31
  16.5 4.5 copy-start.26
  26.4 21.2 %copy-start.27 = (bf16[1,512,1024]{2,1,0:T(8,128)(2,1)S(1)}, bf16[1,512,1024]{2,1,0:T(8,128)(2,1)}, u32[]{:S(2)}) copy-start(bf16[1,512,1024]{2,1,0:T(8,128)(2,1)} %param.9) | copy-start | bytes 3145732
  38.1 34.2 %all-to-all-start = ((bf16[32,2,8192]{2,1,0:T(2,128)(2,1)}), bf16[32,2,8192]{2,1,0:T(2,128)(2,1)}, u32[]{:S(2)}, u32[]{:S(2)}) async-start(bf16[32,2,8192]{2,1,0:T(2,128)(2,1)} %reshape.304), calls=%async_computation | async-start | bytes 2097152 | tf_op jit(solution)/shard_map/all_to_all | solution.py:85
  72.2 33.5 %all-to-all-start.3 = ((bf16[32,2,8192]{2,1,0:T(2,128)(2,1)}), bf16[32,2,8192]{2,1,0:T(2,128)(2,1)}, u32[]{:S(2)}, u32[]{:S(2)}) async-start(bf16[32,2,8192]{2,1,0:T(2,128)(2,1)} %reshape.302), calls=%async_computation.3 | async-start | bytes 2097152 | tf_op jit(solution)/shard_map/all_to_all | solution.py:92
  105.7 81.8 %all-to-all-start.2 = ((bf16[32,3,16,1024]{3,2,1,0:T(8,128)(2,1)}), bf16[32,3,16,1024]{3,2,1,0:T(8,128)(2,1)}, u32[]{:S(2)}, u32[]{:S(2)}) async-start(bf16[32,3,16,1024]{3,2,1,0:T(8,128)(2,1)} %bitcast.218), calls=%async_computation.2 | async-start | bytes 6291456 | tf_op jit(solution)/shard_map/all_to_all | solution.py:102
  187.5 77.3 %all-to-all-start.4 = ((bf16[32,3,16,1024]{3,2,1,0:T(8,128)(2,1)}), bf16[32,3,16,1024]{3,2,1,0:T(8,128)(2,1)}, u32[]{:S(2)}, u32[]{:S(2)}) async-start(bf16[32,3,16,1024]{3,2,1,0:T(8,128)(2,1)} %bitcast.217), calls=%async_computation.4 | async-start | bytes 6291456 | tf_op jit(solution)/shard_map/all_to_all | solution.py:103
  193.5 1.9 copy-start.29
  193.5 3.6 copy-start.32
  195.4 4.2 copy-start.28
  195.4 4.5 copy-start.30
  200.2 3.2 copy-start.19
  200.2 3.2 copy-start.33
  200.9 4.5 copy-start.8
  201.0 8.9 %copy-start.14 = (f32[512,512]{0,1:T(8,128)}, f32[512,512]{0,1:T(8,128)S(1)}, u32[]{:S(2)}) copy-start(f32[512,512]{0,1:T(8,128)S(1)} %fusion.26) | copy-start | bytes 3145732
  275.9 6.3 copy-start.21
  282.2 5.1 copy-start.22
  282.2 10.2 %slice-start = ((s8[8388608]{0:T(1024)(128)(4,1)}), s8[4194304]{0:T(1024)(128)(4,1)S(1)}, s32[]{:S(2)}) async-start(s8[8388608]{0:T(1024)(128)(4,1)} %bitcast.209), calls=%async_computation.9 | async-start | bytes 8388608
  287.3 5.1 slice-start.1
  304.3 3.9 copy-start.2
  304.3 5.8 copy-start.4
  304.3 5.8 copy-start.6
  304.3 6.3 copy-start
  304.3 3.1 copy-start.15
  307.5 2.0 copy-start.17
  318.9 4.0 copy-start.5
  318.9 4.1 copy-start.16
  322.9 8.7 %copy-start.11 = (bf16[8,512,512]{1,2,0:T(8,128)(2,1)}, bf16[8,512,512]{1,2,0:T(8,128)(2,1)S(1)}, u32[]{:S(2)}) copy-start(bf16[8,512,512]{1,2,0:T(8,128)(2,1)S(1)} %fusion.2) | copy-start | bytes 12582916
  322.9 5.1 copy-start.3
  322.9 5.4 copy-start.18
  371.2 100.4 %all-to-all-start.5 = ((bf16[1,3,512,1024]{3,1,0,2:T(4,128)(2,1)}), bf16[1,3,512,1024]{3,1,0,2:T(4,128)(2,1)}, u32[]{:S(2)}, u32[]{:S(2)}) async-start(bf16[1,3,512,1024]{3,1,0,2:T(4,128)(2,1)} %pad_maximum_fusion), calls=%async_computation.5 | async-start | bytes 8388608 | tf_op jit(solution)/shard_map/all_to_all | solution.py:142
  471.6 103.2 %all-to-all-start.7 = ((bf16[1,3,512,1024]{3,1,0,2:T(4,128)(2,1)}), bf16[1,3,512,1024]{3,1,0,2:T(4,128)(2,1)}, u32[]{:S(2)}, u32[]{:S(2)}) async-start(bf16[1,3,512,1024]{3,1,0,2:T(4,128)(2,1)} %pad_maximum_fusion.1), calls=%async_computation.7 | async-start | bytes 8388608 | tf_op jit(solution)/shard_map/all_to_all | solution.py:143
  574.8 33.2 %all-to-all-start.6 = ((bf16[32,16,1024]{2,1,0:T(8,128)(2,1)}), bf16[32,16,1024]{2,1,0:T(8,128)(2,1)}, u32[]{:S(2)}, u32[]{:S(2)}) async-start(bf16[32,16,1024]{2,1,0:T(8,128)(2,1)} %copy.544), calls=%async_computation.6 | async-start | bytes 2097152 | tf_op jit(solution)/shard_map/all_to_all | solution.py:161
  583.2 3.7 copy-start.1
  587.0 1.6 copy-start.9
  587.0 3.7 copy-start.23
  588.6 2.1 copy-start.12
  588.6 3.3 copy-start.7
  588.6 4.5 copy-start.13
  588.6 4.7 copy-start.20
  608.0 116.6 %all-to-all-start.8 = ((bf16[32,16,1024]{2,1,0:T(8,128)(2,1)}), bf16[32,16,1024]{2,1,0:T(8,128)(2,1)S(1)}, u32[]{:S(2)}, u32[]{:S(2)}) async-start(bf16[32,16,1024]{2,1,0:T(8,128)(2,1)} %copy.562), calls=%async_computation.8 | async-start | bytes 2097152 | tf_op jit(solution)/shard_map/all_to_all | solution.py:164
  624.6 6.2 copy-start.25
  637.9 5.3 copy-start.10
  643.2 81.4 %copy-start.24 = (f32[1,512,1024]{2,1,0:T(8,128)S(1)}, f32[1,512,1024]{2,1,0:T(8,128)}, u32[]{:S(2)}) copy-start(f32[1,512,1024]{2,1,0:T(8,128)} %copy.563) | copy-start | bytes 6291460
